TPU v7x, 32 devices: a whole 2x2x4 slice. The times are simulated.
32 devices in a mesh: gz: 8 (over z, x), gy: 4 (over y, core).
Axes of the slice: x: 2, y: 2, z: 4, core: 2. Of those that a mesh axis runs over, the one named last changes fastest.
Arguments:
- volume: bfloat16 [32, 16, 32, 128], P('gz', 'gy'), may hold values from -6 to 6
- kernel_a: bfloat16 [3, 3, 3, 128, 128], replicated, may hold values from -0.109375 to 0.109375
- bias_a: float32 [128], replicated, may hold values from -3 to 3
- kernel_b: bfloat16 [3, 3, 3, 128, 256], P(None, None, None, None, 'gy'), may hold values from -0.109375 to 0.109375
- bias_b: float32 [256], P('gy'), may hold values from -3 to 3
- kernel_c: bfloat16 [3, 3, 3, 256, 512], P(None, None, None, None, 'gy'), may hold values from -0.078125 to 0.078125
- bias_c: float32 [512], P('gy'), may hold values from -3 to 3
Outputs:
- skip_a: bfloat16 [32, 16, 32, 128], P('gz', 'gy')
- skip_b: bfloat16 [16, 8, 16, 256], P('gz', None, None, 'gy')
- bottom: bfloat16 [8, 4, 8, 512], P('gz', None, None, 'gy')
All inputs are finite; a program needn't handle non-finite values.
Results may differ from a plain program's by a relative error of at most 0.0054.
Values may be sent and summed in bfloat16 or wider, within the bound.
A program may use at most 64 MiB of HBM per device.

v0:
```python
import jax
import jax.numpy as jnp
from jax import lax
from jax.sharding import PartitionSpec as P


def extended(array, sides, width):
    for axis, dim in sides:
        peers, length = (lax.axis_size(axis), array.shape[dim])
        up = [(i, (i + 1) % peers) for i in range(peers - 1)]
        down = [(j, i) for i, j in up]
        last = lax.slice_in_dim(array, length - width, length, axis=dim)
        first = lax.slice_in_dim(array, 0, width, axis=dim)
        before = lax.ppermute(last, axis, up)
        after = lax.ppermute(first, axis, down)
        array = jnp.concatenate([before, array, after], axis=dim)
    return array


def conv_relu(padded, kernel, bias):
    out = lax.conv_general_dilated(
        padded[None],
        kernel,
        (1, 1, 1),
        ((0, 0), (0, 0), (1, 1)),
        dimension_numbers=("NDHWC", "DHWIO", "NDHWC"),
        preferred_element_type=jnp.float32,
    )[0]
    return jnp.maximum(out + bias, 0.0).astype(jnp.bfloat16)


def shrink(field):
    depth, height, width, chans = field.shape
    blocks = field.reshape(depth // 2, 2, height // 2, 2, width // 2, 2, chans)
    return jnp.max(blocks, axis=(1, 3, 5))


def pad_height(field):
    return jnp.pad(field, ((0, 0), (1, 1), (0, 0), (0, 0)))


def on_device(volume, kernel_a, bias_a, kernel_b, bias_b, kernel_c, bias_c):
    padded = extended(volume, (("gz", 0), ("gy", 1)), 1)
    skip_a = conv_relu(padded, kernel_a, bias_a)
    pooled_a = shrink(skip_a)
    gathered = lax.all_gather(pooled_a, "gy", axis=1, tiled=True)
    ready_b = extended(gathered, (("gz", 0),), 1)
    skip_b = conv_relu(pad_height(ready_b), kernel_b, bias_b)
    pooled_b = shrink(skip_b)
    widened = lax.all_gather(pooled_b, "gy", axis=3, tiled=True)
    ready_c = extended(widened, (("gz", 0),), 1)
    bottom = conv_relu(pad_height(ready_c), kernel_c, bias_c)
    return (skip_a, skip_b, bottom)


def solution(mesh):
    return jax.shard_map(
        on_device,
        mesh=mesh,
        in_specs=(
            P("gz", "gy", None, None),
            P(),
            P(),
            P(None, None, None, None, "gy"),
            P("gy"),
            P(None, None, None, None, "gy"),
            P("gy"),
        ),
        out_specs=(P("gz", "gy", None, None), P("gz", None, None, "gy"), P("gz", None, None, "gy")),
        check_vma=False,
    )
```

profile of v0, /device:TPU:24, one launch (start us, length us, event | category | flops | bytes accessed | tf_op | source)
XLA Modules:
  0.0 54.5 jit_solution(7939145247504538104)
XLA Ops:
  0.6 0.9 %fusion.45 = (bf16[1,4,32,128]{3,2,1,0:T(8,128)(2,1)S(1)}, bf16[1,4,32,128]{3,2,1,0:T(8,128)(2,1)S(1)}) fusion(bf16[4,4,32,128]{3,2,1,0:T(8,128)(2,1)} %param.7), kind=kLoop, calls=%fused_computation.61 | loop fusion | bytes 131072 | tf_op jit(solution)/shard_map/slice | solution.py:13
  1.6 3.4 %collective-permute-start = (bf16[1,4,32,128]{3,2,1,0:T(8,128)(2,1)S(1)}, bf16[1,4,32,128]{3,2,1,0:T(8,128)(2,1)S(1)}, u32[]{:S(2)}, u32[]{:S(2)}) collective-permute-start(bf16[1,4,32,128]{3,2,1,0:T(8,128)(2,1)S(1)} %get-tuple-element.15), channel_id=1, source_target_pairs={{0,4},{4,8},{8,12},{12,16},{16,20},{20,24},{24,28},{1,5},{5,9},{9,... | collective-permute-start | bytes 98312 | tf_op jit(solution)/shard_map/ppermute | solution.py:14
  5.0 3.3 %collective-permute-start.1 = (bf16[1,4,32,128]{3,2,1,0:T(8,128)(2,1)S(1)}, bf16[1,4,32,128]{3,2,1,0:T(8,128)(2,1)S(1)}, u32[]{:S(2)}, u32[]{:S(2)}) collective-permute-start(bf16[1,4,32,128]{3,2,1,0:T(8,128)(2,1)S(1)} %get-tuple-element.14), channel_id=1, source_target_pairs={{4,0},{8,4},{12,8},{16,12},{20,16},{24,20},{28,24},{5,1},{9,5},{13... | collective-permute-start | bytes 98312 | tf_op jit(solution)/shard_map/ppermute | solution.py:15
  8.3 0.9 %constant_dynamic-update-slice_fusion.1 = bf16[6,4,32,128]{3,2,1,0:T(8,128)(2,1)S(1)} fusion(bf16[6,4,32,128]{3,2,1,0:T(8,128)(2,1)S(1)} %constant_dynamic-update-slice_fusion.2, bf16[4,4,32,128]{3,2,1,0:T(8,128)(2,1)} %param.7), kind=kLoop, calls=%fused_computation.52 | loop fusion | bytes 262144
  9.3 1.5 %collective-permute-done.1 = bf16[1,4,32,128]{3,2,1,0:T(8,128)(2,1)S(1)} collective-permute-done((bf16[1,4,32,128]{3,2,1,0:T(8,128)(2,1)S(1)}, bf16[1,4,32,128]{3,2,1,0:T(8,128)(2,1)S(1)}, u32[]{:S(2)}, u32[]{:S(2)}) %collective-permute-start.1) | collective-permute-done | bytes 32800 | tf_op jit(solution)/shard_map/ppermute | solution.py:15
  10.8 1.4 %collective-permute-start.2 = (bf16[6,1,32,128]{3,2,1,0:T(8,128)(2,1)S(1)}, bf16[6,1,32,128]{3,2,1,0:T(8,128)(2,1)S(1)}, u32[]{:S(2)}, u32[]{:S(2)}) collective-permute-start(bf16[6,1,32,128]{3,2,1,0:T(8,128)(2,1)S(1)} %get-tuple-element.12), channel_id=1, source_target_pairs={{0,1},{1,2},{2,3},{4,5},{5,6},{6,7},{8,9},{9,10},{10,11},{12,13},{... | collective-permute-start | bytes 147464 | tf_op jit(solution)/shard_map/ppermute | solution.py:14
  12.2 1.3 %collective-permute-start.3 = (bf16[6,1,32,128]{3,2,1,0:T(8,128)(2,1)S(1)}, bf16[6,1,32,128]{3,2,1,0:T(8,128)(2,1)S(1)}, u32[]{:S(2)}, u32[]{:S(2)}) collective-permute-start(bf16[6,1,32,128]{3,2,1,0:T(8,128)(2,1)S(1)} %get-tuple-element.13), channel_id=1, source_target_pairs={{1,0},{2,1},{3,2},{5,4},{6,5},{7,6},{9,8},{10,9},{11,10},{13,12},{... | collective-permute-start | bytes 147464 | tf_op jit(solution)/shard_map/ppermute | solution.py:15
  13.5 3.6 %collective-permute-done.3 = bf16[6,1,32,128]{3,2,1,0:T(8,128)(2,1)S(1)} collective-permute-done((bf16[6,1,32,128]{3,2,1,0:T(8,128)(2,1)S(1)}, bf16[6,1,32,128]{3,2,1,0:T(8,128)(2,1)S(1)}, u32[]{:S(2)}, u32[]{:S(2)}) %collective-permute-start.3) | collective-permute-done | bytes 49184 | tf_op jit(solution)/shard_map/ppermute | solution.py:15
  17.2 0.1 copy.50
  17.3 0.1 pad.10.clone
  17.5 1.3 %convolution_select_fusion = f32[4,4,8,5,128]{4,2,3,1,0:T(8,128)S(1)} fusion(bf16[3,3,3,128,128]{4,3,2,1,0:T(8,128)(2,1)S(1)} %copy-done.4, bf16[6,6,1,7,2,128]{5,3,4,1,0,2:T(8,128)(2,1)S(1)} %slice.31, bf16[6,6,1,8,5,128]{5,3,4,1,0,2:T(8,128)(2,1)S(1)} %copy.37, pred[8,5]{0,1:T(8,128)(4,1)S(1)} %copy-done.6), kind=kOutput, calls=%fused_computation | convolution fusion | flops 567861248 | bytes 1710120 | tf_op jit(solution)/shard_map/conv_general_dilated | solution.py:21
  18.9 0.1 copy.38
  19.0 0.2 fusion.31
  19.2 6.7 %all_gather.6 = bf16[2,8,16,128]{3,2,0,1:T(8,128)(2,1)S(1)} all-gather(bf16[2,2,16,128]{3,2,0,1:T(8,128)(2,1)S(1)} %copy.39), channel_id=1, replica_groups=mesh['gz'=8,'gy'=4] {'gy'}, dimensions={1}, use_global_device_ids=true | all-gather | bytes 81920 | tf_op jit(solution)/shard_map/all_gather | solution.py:46
  25.9 1.9 %collective-permute-start.4 = (bf16[1,8,16,128]{3,2,0,1:T(8,128)(2,1)S(1)}, bf16[1,8,16,128]{3,2,0,1:T(8,128)(2,1)S(1)}, u32[]{:S(2)}, u32[]{:S(2)}) collective-permute-start(bf16[1,8,16,128]{3,2,0,1:T(8,128)(2,1)S(1)} %get-tuple-element.16), channel_id=1, source_target_pairs={{0,4},{4,8},{8,12},{12,16},{16,20},{20,24},{24,28},{1,5},{5,9},{9,... | collective-permute-start | bytes 98312 | tf_op jit(solution)/shard_map/ppermute | solution.py:14
  27.9 4.8 %collective-permute-start.5 = (bf16[1,8,16,128]{3,2,0,1:T(8,128)(2,1)S(1)}, bf16[1,8,16,128]{3,2,0,1:T(8,128)(2,1)S(1)}, u32[]{:S(2)}, u32[]{:S(2)}) collective-permute-start(bf16[1,8,16,128]{3,2,0,1:T(8,128)(2,1)S(1)} %get-tuple-element.17), channel_id=1, source_target_pairs={{4,0},{8,4},{12,8},{16,12},{20,16},{24,20},{28,24},{5,1},{9,5},{13... | collective-permute-start | bytes 98312 | tf_op jit(solution)/shard_map/ppermute | solution.py:15
  32.7 0.1 fusion.16
  32.8 0.7 %copy.48 = bf16[4,4,32,128]{3,2,1,0:T(8,128)(2,1)} copy(bf16[4,4,32,128]{3,1,2,0:T(4,128)(2,1)S(1)} %fusion.16) | data formatting | bytes 262144
  33.4 0.8 %collective-permute-done.5 = bf16[1,8,16,128]{3,2,0,1:T(8,128)(2,1)S(1)} collective-permute-done((bf16[1,8,16,128]{3,2,0,1:T(8,128)(2,1)S(1)}, bf16[1,8,16,128]{3,2,0,1:T(8,128)(2,1)S(1)}, u32[]{:S(2)}, u32[]{:S(2)}) %collective-permute-start.5) | collective-permute-done | bytes 32800 | tf_op jit(solution)/shard_map/ppermute | solution.py:15
  34.3 0.1 copy.51
  34.4 0.1 pad.12.clone
  34.6 0.8 %maximum_convert_fusion.1 = (bf16[2,8,8,3,64]{4,2,3,1,0:T(8,128)(2,1)S(1)}, f32[2,8,8,3,64]{4,2,3,1,0:T(8,128)S(1)}) fusion(f32[64]{0:T(128)S(1)} %copy-done.2, bf16[3,3,3,128,64]{3,4,2,1,0:T(8,128)(2,1)S(1)} %copy-done.5, bf16[4,10,1,7,2,128]{5,3,4,1,0,2:T(8,128)(2,1)S(1)} %slice.35, bf16[4,10,1,8,3,128]{5,3,4,1,0,2:T(8,128)(2,1)S(1)} %copy.42, ...), kind=kOutput, calls=%fused_computation.28 | convolution fusion | flops 171196416 | bytes 979224 | tf_op jit(solution)/shard_map/conv_general_dilated | solution.py:21
  35.5 0.1 reduce_max.30
  35.5 0.1 copy.45
  35.7 5.8 %all-gather = bf16[4,8,256]{1,0,2:T(4,128)(2,1)S(1)} all-gather(bf16[4,8,64]{1,0,2:T(4,128)(2,1)S(1)} %copy.45), channel_id=2, replica_groups=mesh['gz'=8,'gy'=4] {'gy'}, dimensions={2}, use_global_device_ids=true | all-gather | bytes 20480 | tf_op jit(solution)/shard_map/all_gather | solution.py:50
  41.5 0.1 copy.46
  41.6 5.1 %collective-permute-start.7 = (bf16[1,4,8,256]{3,2,1,0:T(8,128)(2,1)S(1)}, bf16[1,4,8,256]{3,2,1,0:T(8,128)(2,1)S(1)}, u32[]{:S(2)}, u32[]{:S(2)}) collective-permute-start(bf16[1,4,8,256]{3,2,1,0:T(8,128)(2,1)S(1)} %bitcast.48), channel_id=1, source_target_pairs={{4,0},{8,4},{12,8},{16,12},{20,16},{24,20},{28,24},{5,1},{9,5},{13... | collective-permute-start | bytes 49160 | tf_op jit(solution)/shard_map/ppermute | solution.py:15
  46.7 1.9 %collective-permute-start.6 = (bf16[1,4,8,256]{3,2,1,0:T(8,128)(2,1)S(1)}, bf16[1,4,8,256]{3,2,1,0:T(8,128)(2,1)S(1)}, u32[]{:S(2)}, u32[]{:S(2)}) collective-permute-start(bf16[1,4,8,256]{3,2,1,0:T(8,128)(2,1)S(1)} %bitcast.49), channel_id=1, source_target_pairs={{0,4},{4,8},{8,12},{12,16},{16,20},{20,24},{24,28},{1,5},{5,9},{9,... | collective-permute-start | bytes 49160 | tf_op jit(solution)/shard_map/ppermute | solution.py:14
  48.8 0.6 %copy.49 = bf16[2,8,16,64]{3,2,1,0:T(8,128)(2,1)} copy(bf16[2,8,16,64]{3,1,2,0:T(8,128)(2,1)S(1)} %fusion.30) | data formatting | bytes 65536
  49.4 3.9 %collective-permute-done.6 = bf16[1,4,8,256]{3,2,1,0:T(8,128)(2,1)S(1)} collective-permute-done((bf16[1,4,8,256]{3,2,1,0:T(8,128)(2,1)S(1)}, bf16[1,4,8,256]{3,2,1,0:T(8,128)(2,1)S(1)}, u32[]{:S(2)}, u32[]{:S(2)}) %collective-permute-start.6) | collective-permute-done | bytes 16416 | tf_op jit(solution)/shard_map/ppermute | solution.py:14
  53.3 0.6 %fusion.25 = f32[1,1,4,8,128]{4,0,3,2,1:T(1,128)S(1)} fusion(bf16[3,3,3,256,128]{4,3,2,1,0:T(8,128)(2,1)S(1)} %copy-done, bf16[1,3,6,8,256]{4,3,2,1,0:T(8,128)(2,1)S(1)} %fusion.37), kind=kOutput, calls=%fused_computation.35 | convolution fusion | flops 51904512 | bytes 1859584 | tf_op jit(solution)/shard_map/conv_general_dilated | solution.py:21
  53.9 0.6 %maximum_convert_fusion.2 = bf16[1,4,8,128]{3,2,1,0:T(8,128)(2,1)} fusion(f32[1,4,8,128]{3,2,1,0:T(8,128)S(1)} %bitcast.51, f32[128]{0:T(128)S(1)} %copy-done.3), kind=kLoop, calls=%fused_computation.50 | loop fusion | flops 12288 | bytes 25088 | tf_op jit(solution)/shard_map/convert_element_type | solution.py:29
  (37 shorter events, 0.4 us)
Async XLA Ops:
  0.6 52.6 %copy-start = (bf16[3,3,3,256,128]{4,3,2,1,0:T(8,128)(2,1)S(1)}, bf16[3,3,3,256,128]{4,3,2,1,0:T(8,128)(2,1)}, u32[]{:S(2)}) copy-start(bf16[3,3,3,256,128]{4,3,2,1,0:T(8,128)(2,1)} %param.12) | copy-start | bytes 5308420
  1.6 6.7 %collective-permute-start = (bf16[1,4,32,128]{3,2,1,0:T(8,128)(2,1)S(1)}, bf16[1,4,32,128]{3,2,1,0:T(8,128)(2,1)S(1)}, u32[]{:S(2)}, u32[]{:S(2)}) collective-permute-start(bf16[1,4,32,128]{3,2,1,0:T(8,128)(2,1)S(1)} %get-tuple-element.15), channel_id=1, source_target_pairs={{0,4},{4,8},{8,12},{12,16},{16,20},{20,24},{24,28},{1,5},{5,9},{9,... | collective-permute-start | bytes 98312 | tf_op jit(solution)/shard_map/ppermute | solution.py:14
  5.0 5.8 %collective-permute-start.1 = (bf16[1,4,32,128]{3,2,1,0:T(8,128)(2,1)S(1)}, bf16[1,4,32,128]{3,2,1,0:T(8,128)(2,1)S(1)}, u32[]{:S(2)}, u32[]{:S(2)}) collective-permute-start(bf16[1,4,32,128]{3,2,1,0:T(8,128)(2,1)S(1)} %get-tuple-element.14), channel_id=1, source_target_pairs={{4,0},{8,4},{12,8},{16,12},{20,16},{24,20},{28,24},{5,1},{9,5},{13... | collective-permute-start | bytes 98312 | tf_op jit(solution)/shard_map/ppermute | solution.py:15
  10.8 6.7 %copy-start.4 = (bf16[3,3,3,128,128]{4,3,2,1,0:T(8,128)(2,1)S(1)}, bf16[3,3,3,128,128]{4,3,2,1,0:T(8,128)(2,1)}, u32[]{:S(2)}) copy-start(bf16[3,3,3,128,128]{4,3,2,1,0:T(8,128)(2,1)} %param.8) | copy-start | bytes 2654212
  10.8 6.7 %copy-start.6 = (pred[8,5]{0,1:T(8,128)(4,1)S(1)}, pred[8,5]{0,1:T(8,128)(4,1)}, u32[]{:S(2)}) copy-start(pred[8,5]{0,1:T(8,128)(4,1)} %constant.22) | copy-start | bytes 124
  10.8 2.7 %collective-permute-start.2 = (bf16[6,1,32,128]{3,2,1,0:T(8,128)(2,1)S(1)}, bf16[6,1,32,128]{3,2,1,0:T(8,128)(2,1)S(1)}, u32[]{:S(2)}, u32[]{:S(2)}) collective-permute-start(bf16[6,1,32,128]{3,2,1,0:T(8,128)(2,1)S(1)} %get-tuple-element.12), channel_id=1, source_target_pairs={{0,1},{1,2},{2,3},{4,5},{5,6},{6,7},{8,9},{9,10},{10,11},{12,13},{... | collective-permute-start | bytes 147464 | tf_op jit(solution)/shard_map/ppermute | solution.py:14
  12.2 4.9 %collective-permute-start.3 = (bf16[6,1,32,128]{3,2,1,0:T(8,128)(2,1)S(1)}, bf16[6,1,32,128]{3,2,1,0:T(8,128)(2,1)S(1)}, u32[]{:S(2)}, u32[]{:S(2)}) collective-permute-start(bf16[6,1,32,128]{3,2,1,0:T(8,128)(2,1)S(1)} %get-tuple-element.13), channel_id=1, source_target_pairs={{1,0},{2,1},{3,2},{5,4},{6,5},{7,6},{9,8},{10,9},{11,10},{13,12},{... | collective-permute-start | bytes 147464 | tf_op jit(solution)/shard_map/ppermute | solution.py:15
  17.5 1.5 %copy-start.1 = (f32[128]{0:T(128)S(1)}, f32[128]{0:T(128)}, u32[]{:S(2)}) copy-start(f32[128]{0:T(128)} %param.9) | copy-start | bytes 1540
  18.9 15.6 %copy-start.2 = (f32[64]{0:T(128)S(1)}, f32[64]{0:T(128)}, u32[]{:S(2)}) copy-start(f32[64]{0:T(128)} %param.11) | copy-start | bytes 772
  19.0 15.6 %copy-start.5 = (bf16[3,3,3,128,64]{3,4,2,1,0:T(8,128)(2,1)S(1)}, bf16[3,3,3,128,64]{3,4,2,1,0:T(8,128)(2,1)}, u32[]{:S(2)}) copy-start(bf16[3,3,3,128,64]{3,4,2,1,0:T(8,128)(2,1)} %param.10) | copy-start | bytes 1327108
  19.0 15.6 %copy-start.7 = (pred[8,3]{0,1:T(4,128)(4,1)S(1)}, pred[8,3]{0,1:T(4,128)(4,1)}, u32[]{:S(2)}) copy-start(pred[8,3]{0,1:T(4,128)(4,1)} %constant.23) | copy-start | bytes 76
  25.9 7.5 %collective-permute-start.4 = (bf16[1,8,16,128]{3,2,0,1:T(8,128)(2,1)S(1)}, bf16[1,8,16,128]{3,2,0,1:T(8,128)(2,1)S(1)}, u32[]{:S(2)}, u32[]{:S(2)}) collective-permute-start(bf16[1,8,16,128]{3,2,0,1:T(8,128)(2,1)S(1)} %get-tuple-element.16), channel_id=1, source_target_pairs={{0,4},{4,8},{8,12},{12,16},{16,20},{20,24},{24,28},{1,5},{5,9},{9,... | collective-permute-start | bytes 98312 | tf_op jit(solution)/shard_map/ppermute | solution.py:14
  27.9 6.4 %collective-permute-start.5 = (bf16[1,8,16,128]{3,2,0,1:T(8,128)(2,1)S(1)}, bf16[1,8,16,128]{3,2,0,1:T(8,128)(2,1)S(1)}, u32[]{:S(2)}, u32[]{:S(2)}) collective-permute-start(bf16[1,8,16,128]{3,2,0,1:T(8,128)(2,1)S(1)} %get-tuple-element.17), channel_id=1, source_target_pairs={{4,0},{8,4},{12,8},{16,12},{20,16},{24,20},{28,24},{5,1},{9,5},{13... | collective-permute-start | bytes 98312 | tf_op jit(solution)/shard_map/ppermute | solution.py:15
  41.6 7.8 %collective-permute-start.7 = (bf16[1,4,8,256]{3,2,1,0:T(8,128)(2,1)S(1)}, bf16[1,4,8,256]{3,2,1,0:T(8,128)(2,1)S(1)}, u32[]{:S(2)}, u32[]{:S(2)}) collective-permute-start(bf16[1,4,8,256]{3,2,1,0:T(8,128)(2,1)S(1)} %bitcast.48), channel_id=1, source_target_pairs={{4,0},{8,4},{12,8},{16,12},{20,16},{24,20},{28,24},{5,1},{9,5},{13... | collective-permute-start | bytes 49160 | tf_op jit(solution)/shard_map/ppermute | solution.py:15
  46.7 6.5 %collective-permute-start.6 = (bf16[1,4,8,256]{3,2,1,0:T(8,128)(2,1)S(1)}, bf16[1,4,8,256]{3,2,1,0:T(8,128)(2,1)S(1)}, u32[]{:S(2)}, u32[]{:S(2)}) collective-permute-start(bf16[1,4,8,256]{3,2,1,0:T(8,128)(2,1)S(1)} %bitcast.49), channel_id=1, source_target_pairs={{0,4},{4,8},{8,12},{12,16},{16,20},{20,24},{24,28},{1,5},{5,9},{9,... | collective-permute-start | bytes 49160 | tf_op jit(solution)/shard_map/ppermute | solution.py:14
  48.7 5.2 %copy-start.3 = (f32[128]{0:T(128)S(1)}, f32[128]{0:T(128)}, u32[]{:S(2)}) copy-start(f32[128]{0:T(128)} %param.13) | copy-start | bytes 1540
where the time goes:
time: 54.8 us; the launch traced here: 54.5 us
  starting transfers between devices  23.2 us (42%)
  blocking collectives  12.5 us (23%)
  waiting for transfers between devices  9.79 us (18%)
  local copies, waits for them, and re-layouts  4.2 us (8%)
  matrix products  2.75 us (5%)
  other arithmetic  1.04 us (2%)
  between operations  1.02 us (2%)
    ppermute x4, starting transfers between devices, extended(): after = lax.ppermute(first, axis, down)  14.6 us
    ppermute x4, starting transfers between devices, extended(): before = lax.ppermute(last, axis, up)  8.64 us
    all_gather x1, blocking collectives, on_device(): gathered = lax.all_gather(pooled_a, 'gy', axis=1, tiled=True)  6.7 us
    ppermute x4, waiting for transfers between devices, extended(): after = lax.ppermute(first, axis, down)  5.9 us
    all_gather x1, blocking collectives, on_device(): widened = lax.all_gather(pooled_b, 'gy', axis=3, tiled=True)  5.78 us
    ppermute x4, waiting for transfers between devices, extended(): before = lax.ppermute(last, axis, up)  3.88 us
    conv_general_dilated x3, matrix products, conv_relu(): lax.conv_general_dilated(padded[None], kernel, (1, 1, 1), ((0, 0), (0, 0)...  2.75 us
    unnamed x22, local copies, waits for them, and re-layouts  2.49 us
  transfers between devices with their start and end apart: 8, of which 4 were waited for; matrix products, arithmetic and copies ran while one was open for 4% of the time, Pallas kernels for 0%

commit v1 on v0

--- a/solution.py
+++ b/solution.py
@@ -43,7 +43,12 @@
     padded = extended(volume, (("gz", 0), ("gy", 1)), 1)
     skip_a = conv_relu(padded, kernel_a, bias_a)
     pooled_a = shrink(skip_a)
-    gathered = lax.all_gather(pooled_a, "gy", axis=1, tiled=True)
+    ring = [pooled_a]
+    for hop in range(3):
+        ring.append(lax.ppermute(ring[-1], "gy", [(dev, (dev + 1) % 4) for dev in range(4)]))
+    gathered = jnp.roll(
+        jnp.concatenate(ring[::-1], axis=1), (lax.axis_index("gy") + 1) * ring[0].shape[1], axis=1
+    )
     ready_b = extended(gathered, (("gz", 0),), 1)
     skip_b = conv_relu(pad_height(ready_b), kernel_b, bias_b)
     pooled_b = shrink(skip_b)

time: 54.8 us -> 58.6 us (1.069)
  blocking collectives: 12.5 us -> 7.79 us
  starting transfers between devices: 23.2 us -> 27.6 us
  waiting for transfers between devices: 9.79 us -> 13.5 us
    all_gather x1 -> x0, blocking collectives: 6.7 us -> none  [on_device(): gathered = lax.all_gather(pooled_a, 'gy', axis=1, tiled=True)]
    ppermute x0 -> x3, starting transfers between devices: none -> 4.44 us  [on_device(): lax.ppermute(ring[-1], 'gy', [(dev, (dev + 1) % 4) for dev in range(4)])]
    ppermute x4, waiting for transfers between devices: 5.9 us -> 1.52 us  [extended(): after = lax.ppermute(first, axis, down)]
    ppermute x0 -> x3, waiting for transfers between devices: none -> 4.36 us  [on_device(): lax.ppermute(ring[-1], 'gy', [(dev, (dev + 1) % 4) for dev in range(4)])]
    ppermute x4, waiting for transfers between devices: 3.88 us -> 7.57 us  [extended(): before = lax.ppermute(last, axis, up)]
    ppermute x4, starting transfers between devices: 14.6 us -> 10.9 us  [extended(): after = lax.ppermute(first, axis, down)]
    ppermute x4, starting transfers between devices: 8.64 us -> 12.3 us  [extended(): before = lax.ppermute(last, axis, up)]
    all_gather x1, blocking collectives: 5.78 us -> 7.79 us  [on_device(): widened = lax.all_gather(pooled_b, 'gy', axis=3, tiled=True)]
  transfers between devices with their start and end apart: 8 -> 11, of which waited for: 4 -> 7; matrix products, arithmetic and copies ran while one was open for 4% -> 4% of each run, Pallas kernels for 0% -> 0%
where the time goes in v1:
time: 58.6 us; the launch traced here: 58.2 us
  starting transfers between devices  27.6 us (47%)
  waiting for transfers between devices  13.5 us (23%)
  blocking collectives  7.79 us (13%)
  local copies, waits for them, and re-layouts  4.42 us (8%)
  matrix products  2.75 us (5%)
  other arithmetic  1.14 us (2%)
  between operations  1.02 us (2%)
    ppermute x4, starting transfers between devices, extended(): before = lax.ppermute(last, axis, up)  12.3 us
    ppermute x4, starting transfers between devices, extended(): after = lax.ppermute(first, axis, down)  10.9 us
    all_gather x1, blocking collectives, on_device(): widened = lax.all_gather(pooled_b, 'gy', axis=3, tiled=True)  7.79 us
    ppermute x4, waiting for transfers between devices, extended(): before = lax.ppermute(last, axis, up)  7.57 us
    ppermute x3, starting transfers between devices, on_device(): lax.ppermute(ring[-1], 'gy', [(dev, (dev + 1) % 4) for dev in range(4)])  4.44 us
    ppermute x3, waiting for transfers between devices, on_device(): lax.ppermute(ring[-1], 'gy', [(dev, (dev + 1) % 4) for dev in range(4)])  4.36 us
    conv_general_dilated x3, matrix products, conv_relu(): lax.conv_general_dilated(padded[None], kernel, (1, 1, 1), ((0, 0), (0, 0)...  2.75 us
    unnamed x21, local copies, waits for them, and re-layouts  2.43 us
  transfers between devices with their start and end apart: 11, of which 7 were waited for; matrix products, arithmetic and copies ran while one was open for 4% of the time, Pallas kernels for 0%

profile of v1, /device:TPU:24, one launch (start us, length us, event | category | flops | bytes accessed | tf_op | source)
XLA Modules:
  0.0 58.2 jit_solution(9975243457209307767)
XLA Ops:
  0.6 0.9 %fusion.45 = (bf16[1,4,32,128]{3,2,1,0:T(8,128)(2,1)S(1)}, bf16[1,4,32,128]{3,2,1,0:T(8,128)(2,1)S(1)}) fusion(bf16[4,4,32,128]{3,2,1,0:T(8,128)(2,1)} %param.7), kind=kLoop, calls=%fused_computation.64 | loop fusion | bytes 131072 | tf_op jit(solution)/shard_map/slice | solution.py:13
  1.6 3.4 %collective-permute-start = (bf16[1,4,32,128]{3,2,1,0:T(8,128)(2,1)S(1)}, bf16[1,4,32,128]{3,2,1,0:T(8,128)(2,1)S(1)}, u32[]{:S(2)}, u32[]{:S(2)}) collective-permute-start(bf16[1,4,32,128]{3,2,1,0:T(8,128)(2,1)S(1)} %get-tuple-element.17), channel_id=1, source_target_pairs={{0,4},{4,8},{8,12},{12,16},{16,20},{20,24},{24,28},{1,5},{5,9},{9,... | collective-permute-start | bytes 98312 | tf_op jit(solution)/shard_map/ppermute | solution.py:14
  5.0 3.3 %collective-permute-start.1 = (bf16[1,4,32,128]{3,2,1,0:T(8,128)(2,1)S(1)}, bf16[1,4,32,128]{3,2,1,0:T(8,128)(2,1)S(1)}, u32[]{:S(2)}, u32[]{:S(2)}) collective-permute-start(bf16[1,4,32,128]{3,2,1,0:T(8,128)(2,1)S(1)} %get-tuple-element.16), channel_id=1, source_target_pairs={{4,0},{8,4},{12,8},{16,12},{20,16},{24,20},{28,24},{5,1},{9,5},{13... | collective-permute-start | bytes 98312 | tf_op jit(solution)/shard_map/ppermute | solution.py:15
  8.3 0.9 %constant_dynamic-update-slice_fusion.1 = bf16[6,4,32,128]{3,2,1,0:T(8,128)(2,1)S(1)} fusion(bf16[6,4,32,128]{3,2,1,0:T(8,128)(2,1)S(1)} %constant_dynamic-update-slice_fusion.2, bf16[4,4,32,128]{3,2,1,0:T(8,128)(2,1)} %param.7), kind=kLoop, calls=%fused_computation.52 | loop fusion | bytes 262144
  9.3 1.5 %collective-permute-done.1 = bf16[1,4,32,128]{3,2,1,0:T(8,128)(2,1)S(1)} collective-permute-done((bf16[1,4,32,128]{3,2,1,0:T(8,128)(2,1)S(1)}, bf16[1,4,32,128]{3,2,1,0:T(8,128)(2,1)S(1)}, u32[]{:S(2)}, u32[]{:S(2)}) %collective-permute-start.1) | collective-permute-done | bytes 32800 | tf_op jit(solution)/shard_map/ppermute | solution.py:15
  10.8 1.4 %collective-permute-start.3 = (bf16[6,1,32,128]{3,2,1,0:T(8,128)(2,1)S(1)}, bf16[6,1,32,128]{3,2,1,0:T(8,128)(2,1)S(1)}, u32[]{:S(2)}, u32[]{:S(2)}) collective-permute-start(bf16[6,1,32,128]{3,2,1,0:T(8,128)(2,1)S(1)} %get-tuple-element.13), channel_id=1, source_target_pairs={{1,0},{2,1},{3,2},{5,4},{6,5},{7,6},{9,8},{10,9},{11,10},{13,12},{... | collective-permute-start | bytes 147464 | tf_op jit(solution)/shard_map/ppermute | solution.py:15
  12.2 3.0 %collective-permute-start.2 = (bf16[6,1,32,128]{3,2,1,0:T(8,128)(2,1)S(1)}, bf16[6,1,32,128]{3,2,1,0:T(8,128)(2,1)S(1)}, u32[]{:S(2)}, u32[]{:S(2)}) collective-permute-start(bf16[6,1,32,128]{3,2,1,0:T(8,128)(2,1)S(1)} %get-tuple-element.12), channel_id=1, source_target_pairs={{0,1},{1,2},{2,3},{4,5},{5,6},{6,7},{8,9},{9,10},{10,11},{12,13},{... | collective-permute-start | bytes 147464 | tf_op jit(solution)/shard_map/ppermute | solution.py:14
  15.3 0.9 %collective-permute-done.2 = bf16[6,1,32,128]{3,2,1,0:T(8,128)(2,1)S(1)} collective-permute-done((bf16[6,1,32,128]{3,2,1,0:T(8,128)(2,1)S(1)}, bf16[6,1,32,128]{3,2,1,0:T(8,128)(2,1)S(1)}, u32[]{:S(2)}, u32[]{:S(2)}) %collective-permute-start.2) | collective-permute-done | bytes 49184 | tf_op jit(solution)/shard_map/ppermute | solution.py:14
  16.2 0.1 copy.50
  16.5 1.3 %convolution_select_fusion = f32[4,4,8,5,128]{4,2,3,1,0:T(8,128)S(1)} fusion(bf16[3,3,3,128,128]{4,3,2,1,0:T(8,128)(2,1)S(1)} %copy-done.4, bf16[6,6,1,7,2,128]{5,3,4,1,0,2:T(8,128)(2,1)S(1)} %slice.31, bf16[6,6,1,8,5,128]{5,3,4,1,0,2:T(8,128)(2,1)S(1)} %copy.36, pred[8,5]{0,1:T(8,128)(4,1)S(1)} %copy-done.6), kind=kOutput, calls=%fused_computation | convolution fusion | flops 567861248 | bytes 1710120 | tf_op jit(solution)/shard_map/conv_general_dilated | solution.py:21
  18.0 0.2 fusion.31
  18.2 1.5 %collective-permute-start.4 = (bf16[2,2,16,128]{3,1,2,0:T(2,128)(2,1)S(1)}, bf16[2,2,16,128]{3,1,2,0:T(2,128)(2,1)S(1)}, u32[]{:S(2)}, u32[]{:S(2)}) collective-permute-start(bf16[2,2,16,128]{3,1,2,0:T(2,128)(2,1)S(1)} %fusion.31), channel_id=1, source_target_pairs={{0,1},{1,2},{2,3},{3,0},{4,5},{5,6},{6,7},{7,4},{8,9},{9,10},{10,1... | collective-permute-start | bytes 49160 | tf_op jit(solution)/shard_map/ppermute | solution.py:48
  19.7 1.7 %collective-permute-done.4 = bf16[2,2,16,128]{3,1,2,0:T(2,128)(2,1)S(1)} collective-permute-done((bf16[2,2,16,128]{3,1,2,0:T(2,128)(2,1)S(1)}, bf16[2,2,16,128]{3,1,2,0:T(2,128)(2,1)S(1)}, u32[]{:S(2)}, u32[]{:S(2)}) %collective-permute-start.4) | collective-permute-done | bytes 16416 | tf_op jit(solution)/shard_map/ppermute | solution.py:48
  21.5 1.5 %collective-permute-start.5 = (bf16[2,2,16,128]{3,1,2,0:T(2,128)(2,1)S(1)}, bf16[2,2,16,128]{3,1,2,0:T(2,128)(2,1)S(1)}, u32[]{:S(2)}, u32[]{:S(2)}) collective-permute-start(bf16[2,2,16,128]{3,1,2,0:T(2,128)(2,1)S(1)} %collective-permute-done.4), channel_id=1, source_target_pairs={{0,1},{1,2},{2,3},{3,0},{4,5},{5,6},{6,7},{7,4},{8,9},{9,10},{10,1... | collective-permute-start | bytes 49160 | tf_op jit(solution)/shard_map/ppermute | solution.py:48
  22.9 1.7 %collective-permute-done.5 = bf16[2,2,16,128]{3,1,2,0:T(2,128)(2,1)S(1)} collective-permute-done((bf16[2,2,16,128]{3,1,2,0:T(2,128)(2,1)S(1)}, bf16[2,2,16,128]{3,1,2,0:T(2,128)(2,1)S(1)}, u32[]{:S(2)}, u32[]{:S(2)}) %collective-permute-start.5) | collective-permute-done | bytes 16416 | tf_op jit(solution)/shard_map/ppermute | solution.py:48
  24.6 1.5 %collective-permute-start.6 = (bf16[2,2,16,128]{3,1,2,0:T(2,128)(2,1)S(1)}, bf16[2,2,16,128]{3,1,2,0:T(2,128)(2,1)S(1)}, u32[]{:S(2)}, u32[]{:S(2)}) collective-permute-start(bf16[2,2,16,128]{3,1,2,0:T(2,128)(2,1)S(1)} %collective-permute-done.5), channel_id=1, source_target_pairs={{0,1},{1,2},{2,3},{3,0},{4,5},{5,6},{6,7},{7,4},{8,9},{9,10},{10,1... | collective-permute-start | bytes 49160 | tf_op jit(solution)/shard_map/ppermute | solution.py:48
  26.2 0.7 %copy.46 = bf16[4,4,32,128]{3,2,1,0:T(8,128)(2,1)} copy(bf16[4,4,32,128]{3,1,2,0:T(4,128)(2,1)S(1)} %fusion.22) | data formatting | bytes 262144
  26.8 0.9 %collective-permute-done.6 = bf16[2,2,16,128]{3,1,2,0:T(2,128)(2,1)S(1)} collective-permute-done((bf16[2,2,16,128]{3,1,2,0:T(2,128)(2,1)S(1)}, bf16[2,2,16,128]{3,1,2,0:T(2,128)(2,1)S(1)}, u32[]{:S(2)}, u32[]{:S(2)}) %collective-permute-start.6) | collective-permute-done | bytes 16416 | tf_op jit(solution)/shard_map/ppermute | solution.py:48
  27.8 0.2 concatenate.20
  28.1 4.2 %collective-permute-start.8 = (bf16[1,8,16,128]{3,1,2,0:T(8,128)(2,1)S(1)}, bf16[1,8,16,128]{3,1,2,0:T(8,128)(2,1)S(1)}, u32[]{:S(2)}, u32[]{:S(2)}) collective-permute-start(bf16[1,8,16,128]{3,1,2,0:T(8,128)(2,1)S(1)} %get-tuple-element.15), channel_id=1, source_target_pairs={{4,0},{8,4},{12,8},{16,12},{20,16},{24,20},{28,24},{5,1},{9,5},{13... | collective-permute-start | bytes 98312 | tf_op jit(solution)/shard_map/ppermute | solution.py:15
  32.3 1.9 %collective-permute-start.7 = (bf16[1,8,16,128]{3,1,2,0:T(8,128)(2,1)S(1)}, bf16[1,8,16,128]{3,1,2,0:T(8,128)(2,1)S(1)}, u32[]{:S(2)}, u32[]{:S(2)}) collective-permute-start(bf16[1,8,16,128]{3,1,2,0:T(8,128)(2,1)S(1)} %get-tuple-element.14), channel_id=1, source_target_pairs={{0,4},{4,8},{8,12},{12,16},{16,20},{20,24},{24,28},{1,5},{5,9},{9,... | collective-permute-start | bytes 98312 | tf_op jit(solution)/shard_map/ppermute | solution.py:14
  34.3 4.8 %collective-permute-done.7 = bf16[1,8,16,128]{3,1,2,0:T(8,128)(2,1)S(1)} collective-permute-done((bf16[1,8,16,128]{3,1,2,0:T(8,128)(2,1)S(1)}, bf16[1,8,16,128]{3,1,2,0:T(8,128)(2,1)S(1)}, u32[]{:S(2)}, u32[]{:S(2)}) %collective-permute-start.7) | collective-permute-done | bytes 32800 | tf_op jit(solution)/shard_map/ppermute | solution.py:14
  39.5 0.8 %maximum_convert_fusion.1 = (bf16[2,8,8,3,64]{4,2,3,1,0:T(8,128)(2,1)S(1)}, f32[2,8,8,3,64]{4,2,3,1,0:T(8,128)S(1)}) fusion(f32[64]{0:T(128)S(1)} %copy-done.2, bf16[3,3,3,128,64]{3,4,2,1,0:T(8,128)(2,1)S(1)} %copy-done.5, bf16[4,10,1,7,2,128]{5,3,4,1,0,2:T(8,128)(2,1)S(1)} %slice.33, bf16[4,10,1,8,3,128]{5,3,4,1,0,2:T(8,128)(2,1)S(1)} %copy.40, ...), kind=kOutput, calls=%fused_computation.34 | convolution fusion | flops 171196416 | bytes 979224 | tf_op jit(solution)/shard_map/conv_general_dilated | solution.py:21
  40.5 0.1 copy.43
  40.6 7.8 %all-gather = bf16[4,8,256]{1,0,2:T(4,128)(2,1)S(1)} all-gather(bf16[4,8,64]{1,0,2:T(4,128)(2,1)S(1)} %copy.43), channel_id=2, replica_groups=mesh['gz'=8,'gy'=4] {'gy'}, dimensions={2}, use_global_device_ids=true | all-gather | bytes 20480 | tf_op jit(solution)/shard_map/all_gather | solution.py:55
  48.4 0.1 copy.44
  48.5 1.9 %collective-permute-start.10 = (bf16[1,4,8,256]{3,2,1,0:T(8,128)(2,1)S(1)}, bf16[1,4,8,256]{3,2,1,0:T(8,128)(2,1)S(1)}, u32[]{:S(2)}, u32[]{:S(2)}) collective-permute-start(bf16[1,4,8,256]{3,2,1,0:T(8,128)(2,1)S(1)} %bitcast.48), channel_id=1, source_target_pairs={{4,0},{8,4},{12,8},{16,12},{20,16},{24,20},{28,24},{5,1},{9,5},{13... | collective-permute-start | bytes 49160 | tf_op jit(solution)/shard_map/ppermute | solution.py:15
  50.5 3.9 %collective-permute-start.9 = (bf16[1,4,8,256]{3,2,1,0:T(8,128)(2,1)S(1)}, bf16[1,4,8,256]{3,2,1,0:T(8,128)(2,1)S(1)}, u32[]{:S(2)}, u32[]{:S(2)}) collective-permute-start(bf16[1,4,8,256]{3,2,1,0:T(8,128)(2,1)S(1)} %bitcast.49), channel_id=1, source_target_pairs={{0,4},{4,8},{8,12},{12,16},{16,20},{20,24},{24,28},{1,5},{5,9},{9,... | collective-permute-start | bytes 49160 | tf_op jit(solution)/shard_map/ppermute | solution.py:14
  54.5 0.6 %copy.47 = bf16[2,8,16,64]{3,2,1,0:T(8,128)(2,1)} copy(bf16[2,8,16,64]{3,1,2,0:T(8,128)(2,1)S(1)} %fusion.30) | data formatting | bytes 65536
  55.1 1.9 %collective-permute-done.9 = bf16[1,4,8,256]{3,2,1,0:T(8,128)(2,1)S(1)} collective-permute-done((bf16[1,4,8,256]{3,2,1,0:T(8,128)(2,1)S(1)}, bf16[1,4,8,256]{3,2,1,0:T(8,128)(2,1)S(1)}, u32[]{:S(2)}, u32[]{:S(2)}) %collective-permute-start.9) | collective-permute-done | bytes 16416 | tf_op jit(solution)/shard_map/ppermute | solution.py:14
  57.0 0.6 fusion.25
  57.6 0.6 %maximum_convert_fusion.2 = bf16[1,4,8,128]{3,2,1,0:T(8,128)(2,1)} fusion(f32[1,4,8,128]{3,2,1,0:T(8,128)S(1)} %bitcast.51, f32[128]{0:T(128)S(1)} %copy-done.3), kind=kLoop, calls=%fused_computation.50 | loop fusion | flops 12288 | bytes 25088 | tf_op jit(solution)/shard_map/convert_element_type | solution.py:29
  (42 shorter events, 1.0 us)
Async XLA Ops:
  0.6 56.4 %copy-start = (bf16[3,3,3,256,128]{4,3,2,1,0:T(8,128)(2,1)S(1)}, bf16[3,3,3,256,128]{4,3,2,1,0:T(8,128)(2,1)}, u32[]{:S(2)}) copy-start(bf16[3,3,3,256,128]{4,3,2,1,0:T(8,128)(2,1)} %param.12) | copy-start | bytes 5308420
  1.6 6.7 %collective-permute-start = (bf16[1,4,32,128]{3,2,1,0:T(8,128)(2,1)S(1)}, bf16[1,4,32,128]{3,2,1,0:T(8,128)(2,1)S(1)}, u32[]{:S(2)}, u32[]{:S(2)}) collective-permute-start(bf16[1,4,32,128]{3,2,1,0:T(8,128)(2,1)S(1)} %get-tuple-element.17), channel_id=1, source_target_pairs={{0,4},{4,8},{8,12},{12,16},{16,20},{20,24},{24,28},{1,5},{5,9},{9,... | collective-permute-start | bytes 98312 | tf_op jit(solution)/shard_map/ppermute | solution.py:14
  5.0 5.8 %collective-permute-start.1 = (bf16[1,4,32,128]{3,2,1,0:T(8,128)(2,1)S(1)}, bf16[1,4,32,128]{3,2,1,0:T(8,128)(2,1)S(1)}, u32[]{:S(2)}, u32[]{:S(2)}) collective-permute-start(bf16[1,4,32,128]{3,2,1,0:T(8,128)(2,1)S(1)} %get-tuple-element.16), channel_id=1, source_target_pairs={{4,0},{8,4},{12,8},{16,12},{20,16},{24,20},{28,24},{5,1},{9,5},{13... | collective-permute-start | bytes 98312 | tf_op jit(solution)/shard_map/ppermute | solution.py:15
  10.8 5.7 %copy-start.4 = (bf16[3,3,3,128,128]{4,3,2,1,0:T(8,128)(2,1)S(1)}, bf16[3,3,3,128,128]{4,3,2,1,0:T(8,128)(2,1)}, u32[]{:S(2)}) copy-start(bf16[3,3,3,128,128]{4,3,2,1,0:T(8,128)(2,1)} %param.8) | copy-start | bytes 2654212
  10.8 5.8 %copy-start.6 = (pred[8,5]{0,1:T(8,128)(4,1)S(1)}, pred[8,5]{0,1:T(8,128)(4,1)}, u32[]{:S(2)}) copy-start(pred[8,5]{0,1:T(8,128)(4,1)} %constant.52) | copy-start | bytes 124
  10.8 4.5 %collective-permute-start.3 = (bf16[6,1,32,128]{3,2,1,0:T(8,128)(2,1)S(1)}, bf16[6,1,32,128]{3,2,1,0:T(8,128)(2,1)S(1)}, u32[]{:S(2)}, u32[]{:S(2)}) collective-permute-start(bf16[6,1,32,128]{3,2,1,0:T(8,128)(2,1)S(1)} %get-tuple-element.13), channel_id=1, source_target_pairs={{1,0},{2,1},{3,2},{5,4},{6,5},{7,6},{9,8},{10,9},{11,10},{13,12},{... | collective-permute-start | bytes 147464 | tf_op jit(solution)/shard_map/ppermute | solution.py:15
  12.2 3.9 %collective-permute-start.2 = (bf16[6,1,32,128]{3,2,1,0:T(8,128)(2,1)S(1)}, bf16[6,1,32,128]{3,2,1,0:T(8,128)(2,1)S(1)}, u32[]{:S(2)}, u32[]{:S(2)}) collective-permute-start(bf16[6,1,32,128]{3,2,1,0:T(8,128)(2,1)S(1)} %get-tuple-element.12), channel_id=1, source_target_pairs={{0,1},{1,2},{2,3},{4,5},{5,6},{6,7},{8,9},{9,10},{10,11},{12,13},{... | collective-permute-start | bytes 147464 | tf_op jit(solution)/shard_map/ppermute | solution.py:14
  16.5 1.5 %copy-start.1 = (f32[128]{0:T(128)S(1)}, f32[128]{0:T(128)}, u32[]{:S(2)}) copy-start(f32[128]{0:T(128)} %param.9) | copy-start | bytes 1540
  18.0 21.5 %copy-start.2 = (f32[64]{0:T(128)S(1)}, f32[64]{0:T(128)}, u32[]{:S(2)}) copy-start(f32[64]{0:T(128)} %param.11) | copy-start | bytes 772
  18.0 21.5 %copy-start.5 = (bf16[3,3,3,128,64]{3,4,2,1,0:T(8,128)(2,1)S(1)}, bf16[3,3,3,128,64]{3,4,2,1,0:T(8,128)(2,1)}, u32[]{:S(2)}) copy-start(bf16[3,3,3,128,64]{3,4,2,1,0:T(8,128)(2,1)} %param.10) | copy-start | bytes 1327108
  18.0 21.5 %copy-start.7 = (pred[8,3]{0,1:T(4,128)(4,1)S(1)}, pred[8,3]{0,1:T(4,128)(4,1)}, u32[]{:S(2)}) copy-start(pred[8,3]{0,1:T(4,128)(4,1)} %constant.53) | copy-start | bytes 76
  18.2 3.2 %collective-permute-start.4 = (bf16[2,2,16,128]{3,1,2,0:T(2,128)(2,1)S(1)}, bf16[2,2,16,128]{3,1,2,0:T(2,128)(2,1)S(1)}, u32[]{:S(2)}, u32[]{:S(2)}) collective-permute-start(bf16[2,2,16,128]{3,1,2,0:T(2,128)(2,1)S(1)} %fusion.31), channel_id=1, source_target_pairs={{0,1},{1,2},{2,3},{3,0},{4,5},{5,6},{6,7},{7,4},{8,9},{9,10},{10,1... | collective-permute-start | bytes 49160 | tf_op jit(solution)/shard_map/ppermute | solution.py:48
  21.5 3.2 %collective-permute-start.5 = (bf16[2,2,16,128]{3,1,2,0:T(2,128)(2,1)S(1)}, bf16[2,2,16,128]{3,1,2,0:T(2,128)(2,1)S(1)}, u32[]{:S(2)}, u32[]{:S(2)}) collective-permute-start(bf16[2,2,16,128]{3,1,2,0:T(2,128)(2,1)S(1)} %collective-permute-done.4), channel_id=1, source_target_pairs={{0,1},{1,2},{2,3},{3,0},{4,5},{5,6},{6,7},{7,4},{8,9},{9,10},{10,1... | collective-permute-start | bytes 49160 | tf_op jit(solution)/shard_map/ppermute | solution.py:48
  24.6 3.2 %collective-permute-start.6 = (bf16[2,2,16,128]{3,1,2,0:T(2,128)(2,1)S(1)}, bf16[2,2,16,128]{3,1,2,0:T(2,128)(2,1)S(1)}, u32[]{:S(2)}, u32[]{:S(2)}) collective-permute-start(bf16[2,2,16,128]{3,1,2,0:T(2,128)(2,1)S(1)} %collective-permute-done.5), channel_id=1, source_target_pairs={{0,1},{1,2},{2,3},{3,0},{4,5},{5,6},{6,7},{7,4},{8,9},{9,10},{10,1... | collective-permute-start | bytes 49160 | tf_op jit(solution)/shard_map/ppermute | solution.py:48
  28.1 6.2 %collective-permute-start.8 = (bf16[1,8,16,128]{3,1,2,0:T(8,128)(2,1)S(1)}, bf16[1,8,16,128]{3,1,2,0:T(8,128)(2,1)S(1)}, u32[]{:S(2)}, u32[]{:S(2)}) collective-permute-start(bf16[1,8,16,128]{3,1,2,0:T(8,128)(2,1)S(1)} %get-tuple-element.15), channel_id=1, source_target_pairs={{4,0},{8,4},{12,8},{16,12},{20,16},{24,20},{28,24},{5,1},{9,5},{13... | collective-permute-start | bytes 98312 | tf_op jit(solution)/shard_map/ppermute | solution.py:15
  32.3 6.8 %collective-permute-start.7 = (bf16[1,8,16,128]{3,1,2,0:T(8,128)(2,1)S(1)}, bf16[1,8,16,128]{3,1,2,0:T(8,128)(2,1)S(1)}, u32[]{:S(2)}, u32[]{:S(2)}) collective-permute-start(bf16[1,8,16,128]{3,1,2,0:T(8,128)(2,1)S(1)} %get-tuple-element.14), channel_id=1, source_target_pairs={{0,4},{4,8},{8,12},{12,16},{16,20},{20,24},{24,28},{1,5},{5,9},{9,... | collective-permute-start | bytes 98312 | tf_op jit(solution)/shard_map/ppermute | solution.py:14
  48.5 6.6 %collective-permute-start.10 = (bf16[1,4,8,256]{3,2,1,0:T(8,128)(2,1)S(1)}, bf16[1,4,8,256]{3,2,1,0:T(8,128)(2,1)S(1)}, u32[]{:S(2)}, u32[]{:S(2)}) collective-permute-start(bf16[1,4,8,256]{3,2,1,0:T(8,128)(2,1)S(1)} %bitcast.48), channel_id=1, source_target_pairs={{4,0},{8,4},{12,8},{16,12},{20,16},{24,20},{28,24},{5,1},{9,5},{13... | collective-permute-start | bytes 49160 | tf_op jit(solution)/shard_map/ppermute | solution.py:15
  50.5 6.5 %collective-permute-start.9 = (bf16[1,4,8,256]{3,2,1,0:T(8,128)(2,1)S(1)}, bf16[1,4,8,256]{3,2,1,0:T(8,128)(2,1)S(1)}, u32[]{:S(2)}, u32[]{:S(2)}) collective-permute-start(bf16[1,4,8,256]{3,2,1,0:T(8,128)(2,1)S(1)} %bitcast.49), channel_id=1, source_target_pairs={{0,4},{4,8},{8,12},{12,16},{16,20},{20,24},{24,28},{1,5},{5,9},{9,... | collective-permute-start | bytes 49160 | tf_op jit(solution)/shard_map/ppermute | solution.py:14
  54.4 3.2 %copy-start.3 = (f32[128]{0:T(128)S(1)}, f32[128]{0:T(128)}, u32[]{:S(2)}) copy-start(f32[128]{0:T(128)} %param.13) | copy-start | bytes 1540
